TPU v7x, 32 devices: a whole 2x2x4 slice. The times are simulated.
32 devices in a mesh: mem: 8 (over z, y), lat: 4 (over x, core).
Axes of the slice: x: 2, y: 2, z: 4, core: 2. Of those that a mesh axis runs over, the one named last changes fastest.
Arguments:
- prior_sample_states: bfloat16 [16, 2, 16, 1024], P('mem', None, 'lat'), may hold values from -6 to 6
- wind_cfl_ratios: float32 [2, 16, 1024], P(None, 'lat'), may hold values from -0.45 to 0.45
- obs_cell: int32 [4, 2048], P('lat', 'mem'), may hold values from 0 to 511
- obs_value: float32 [4, 2048], P('lat', 'mem'), may hold values from -6 to 6
- obs_precision: float32 [4, 2048], P('lat', 'mem'), may hold values from 0.25 to 4
- neighbours: int32 [16, 8, 512], P('lat', 'mem'), may hold values from 0 to 1279, as said below
- obs_counts: int32 [16, 8], P('lat', 'mem'), may hold values from 128 to 512, as said below
Outputs:
- analysis: bfloat16 [16, 2, 16, 1024], P('mem', None, 'lat')
Inputs may be any that keep to these rules, and one draw needn't show every extreme that they name: `obs_counts`: in every tile some block's list has all 512 slots live. `neighbours`: the 512 entries of one list are distinct and index the extended set of its tile.
All inputs are finite; a program needn't handle non-finite values. Where the computation divides by a largest or mean magnitude, that divisor is 1e-20 or more.
Results may differ from a plain program's by a relative error of at most 0.0053.
Values may be sent and summed in bfloat16 or wider, within the bound.
A program may use at most 64 MiB of HBM per device.

v0:
```python
import jax
import jax.numpy as jnp
from jax import lax
from jax.sharding import PartitionSpec as P

PATCH_WIDTH = 128
SECTIONS = 4
NS_ITERS = 6
LOC_ROWS = 2
LOC_COLS = 64
KAPPA = (0.025, 0.0125)
HIGHEST = lax.Precision.HIGHEST


def with_halo(cells, sides, width):
    for axis, dim in sides:
        count = lax.axis_size(axis)
        ends = count - 1
        head = lax.slice_in_dim(cells, 0, width, axis=dim)
        tail = lax.slice_in_dim(cells, cells.shape[dim] - width, cells.shape[dim], axis=dim)
        cells = jnp.concatenate(
            [
                lax.ppermute(tail, axis, [(i, (i + 1) % count) for i in range(ends)]),
                cells,
                lax.ppermute(head, axis, [((i + 1) % count, i) for i in range(ends)]),
            ],
            axis=dim,
        )
    return cells


def advance(padded, east_wind, north_wind, diffusion):
    centre = padded[:, 1:-1, :]
    north_row = padded[:, 2:, :]
    south_row = padded[:, :-2, :]
    widened = jnp.pad(centre, ((0, 0), (0, 0), (1, 1)))
    west_cell = widened[:, :, :-2]
    east_cell = widened[:, :, 2:]
    transport = (
        jnp.maximum(east_wind, 0.0) * (centre - west_cell)
        + jnp.minimum(east_wind, 0.0) * (east_cell - centre)
        + jnp.maximum(north_wind, 0.0) * (centre - south_row)
        + jnp.minimum(north_wind, 0.0) * (north_row - centre)
    )
    return (
        centre
        - transport
        + diffusion * (north_row + south_row + east_cell + west_cell - 4.0 * centre)
    )


def place_piece(piece, sample_realizations, row_shift, col_shift):
    return jnp.concatenate(
        [
            piece[: sample_realizations + 2],
            piece[sample_realizations + 2 : sample_realizations + 3] + row_shift,
            piece[sample_realizations + 3 :] + col_shift,
        ],
        axis=0,
    )


def analyze(mesh_patch, extended, block_lists, block_counts):
    sample_realizations = mesh_patch.shape[0]
    analysis_block_count = mesh_patch.shape[2]
    tile_width = mesh_patch.shape[3]
    extent = extended.shape[1]
    slot_count = block_lists.shape[1]
    obs_ens = extended[:sample_realizations]
    obs_mean = jnp.mean(obs_ens, axis=0)
    spread = obs_ens - obs_mean
    innovation = extended[sample_realizations] - obs_mean
    precision = extended[sample_realizations + 1]
    obs_row = extended[sample_realizations + 2]
    obs_col = extended[sample_realizations + 3]
    active = (jnp.arange(slot_count, dtype=jnp.int32)[None, :] < block_counts[:, None]).astype(
        jnp.float32
    )
    block_ids = jnp.broadcast_to(
        jnp.arange(analysis_block_count, dtype=jnp.int32)[:, None], block_lists.shape
    )
    membership = (
        jnp.zeros((analysis_block_count, extent), jnp.float32)
        .at[block_ids, block_lists]
        .set(active)
    )
    block_row = jnp.arange(analysis_block_count, dtype=jnp.float32)[:, None]
    row_gap = obs_row[None, :] - block_row
    col_gap = obs_col[None, :] - 0.5 * (tile_width - 1)
    tapering = jnp.exp(-0.5 * ((row_gap / LOC_ROWS) ** 2 + (col_gap / LOC_COLS) ** 2))
    weight = membership * tapering * precision[None, :]
    weighted = spread[None, :, :] * weight[:, None, :]
    gram_matrix = jnp.einsum("rek,fk->ref", weighted, spread, precision=HIGHEST)
    forcing = jnp.einsum("ek,rk->re", spread, weight * innovation[None, :], precision=HIGHEST)
    identity = jnp.eye(sample_realizations, dtype=jnp.float32)
    system = (sample_realizations - 1.0) * identity + gram_matrix
    bounds = sample_realizations - 1.0 + jnp.max(jnp.sum(jnp.abs(gram_matrix), axis=2), axis=1)
    upper_iter = system / bounds[:, None, None]
    lower_iter = jnp.broadcast_to(identity, system.shape)
    for iteration in range(NS_ITERS):
        factor = 1.5 * identity - 0.5 * jnp.einsum(
            "rij,rjk->rik", lower_iter, upper_iter, precision=HIGHEST
        )
        upper_iter = jnp.einsum("rij,rjk->rik", upper_iter, factor, precision=HIGHEST)
        lower_iter = jnp.einsum("rij,rjk->rik", factor, lower_iter, precision=HIGHEST)
    inv_root = lower_iter / jnp.sqrt(bounds)[:, None, None]
    half_shift = jnp.einsum("rij,rj->ri", inv_root, forcing, precision=HIGHEST)
    mean_shift = jnp.einsum("rij,rj->ri", inv_root, half_shift, precision=HIGHEST)
    weights = jnp.sqrt(sample_realizations - 1.0) * inv_root + mean_shift[:, :, None]
    fields = mesh_patch.astype(jnp.float32)
    centre = jnp.mean(fields, axis=0)
    anomalies = fields - centre
    updated = centre + jnp.einsum("kvrc,rkm->mvrc", anomalies, weights, precision=HIGHEST)
    return updated.astype(jnp.bfloat16)


def on_device(
    prior_sample_states, wind_cfl_ratios, obs_cell, obs_value, obs_precision, neighbours, obs_counts
):
    ensemble_count = prior_sample_states.shape[0]
    analysis_block_count = prior_sample_states.shape[2]
    longitude_index = prior_sample_states.shape[3]
    present_states = prior_sample_states.astype(jnp.float32).reshape(
        ensemble_count * 2, analysis_block_count, longitude_index
    )
    diffusion = jnp.tile(jnp.array(KAPPA, jnp.float32).reshape(2, 1, 1), (ensemble_count, 1, 1))
    for section_index in range(SECTIONS):
        padded = with_halo(present_states, (("lat", 1),), 1)
        present_states = advance(padded, wind_cfl_ratios[0], wind_cfl_ratios[1], diffusion)
    predict_advance = present_states.astype(jnp.bfloat16).reshape(
        ensemble_count, 2, analysis_block_count, longitude_index
    )
    cells = obs_cell[0]
    own_meta = jnp.stack(
        [
            obs_value[0],
            obs_precision[0],
            (cells // PATCH_WIDTH).astype(jnp.float32),
            (cells % PATCH_WIDTH).astype(jnp.float32),
        ],
        axis=0,
    )
    mesh_patches = lax.all_to_all(predict_advance, "mem", split_axis=3, concat_axis=0, tiled=True)
    sample_realizations = mesh_patches.shape[0]
    own_obs = jnp.take(mesh_patches[:, 0].reshape(sample_realizations, -1), cells, axis=1).astype(
        jnp.float32
    )
    combined = jnp.concatenate([own_obs, own_meta], axis=0)
    beside_all = with_halo(combined[None, None], (("mem", 1), ("lat", 0)), 1)
    pieces = [
        beside_all[1, 1],
        beside_all[0, 1],
        beside_all[2, 1],
        beside_all[1, 0],
        beside_all[1, 2],
    ]
    row_span = float(analysis_block_count)
    col_span = float(PATCH_WIDTH)
    shifts = [(0.0, 0.0), (-row_span, 0.0), (row_span, 0.0), (0.0, -col_span), (0.0, col_span)]
    extended = jnp.concatenate(
        [
            place_piece(pieces[slot], sample_realizations, shifts[slot][0], shifts[slot][1])
            for slot in range(5)
        ],
        axis=1,
    )
    updated = analyze(mesh_patches, extended, neighbours[:, 0, :], obs_counts[:, 0])
    return lax.all_to_all(updated, "mem", split_axis=0, concat_axis=3, tiled=True)


def solution(mesh):
    placed = (
        P("mem", None, "lat", None),
        P(None, "lat", None),
        P("lat", "mem"),
        P("lat", "mem"),
        P("lat", "mem"),
        P("lat", "mem", None),
        P("lat", "mem"),
    )
    return jax.shard_map(
        on_device,
        mesh=mesh,
        in_specs=placed,
        out_specs=P("mem", None, "lat", None),
        check_vma=False,
    )
```

profile of v0, /device:TPU:1, one launch (start us, length us, event | category | flops | bytes accessed | tf_op | source)
XLA Modules:
  0.0 93.3 jit_solution(944328057822813094)
XLA Ops:
  0.0 0.8 bitcast_convert_fusion
  0.8 4.5 %collective-permute-start = (f32[4,1,1024]{2,0,1:T(4,128)S(1)}, f32[4,1,1024]{2,0,1:T(4,128)S(1)}, u32[]{:S(2)}, u32[]{:S(2)}) collective-permute-start(f32[4,1,1024]{2,0,1:T(4,128)S(1)} %get-tuple-element.17), channel_id=1, source_target_pairs={{0,1},{1,2},{2,3},{4,5},{5,6},{6,7},{8,9},{9,10},{10,11},{12,13},{... | collective-permute-start | bytes 49160 | tf_op jit(solution)/shard_map/ppermute | solution.py:23
  5.4 1.9 %collective-permute-start.1 = (f32[4,1,1024]{2,0,1:T(4,128)S(1)}, f32[4,1,1024]{2,0,1:T(4,128)S(1)}, u32[]{:S(2)}, u32[]{:S(2)}) collective-permute-start(f32[4,1,1024]{2,0,1:T(4,128)S(1)} %get-tuple-element.18), channel_id=1, source_target_pairs={{1,0},{2,1},{3,2},{5,4},{6,5},{7,6},{9,8},{10,9},{11,10},{13,12},{... | collective-permute-start | bytes 49160 | tf_op jit(solution)/shard_map/ppermute | solution.py:25
  7.4 0.6 copy-done.2
  8.1 0.6 copy-done.6
  8.7 0.1 multiply_reduce_fusion
  8.8 0.6 copy-done.7
  9.4 0.1 and_reduce_fusion
  9.5 0.6 copy-done.5
  10.2 0.6 copy-done.8
  11.0 0.1 fusion.58
  11.1 3.6 %collective-permute-start.2 = (f32[4,1,1024]{2,0,1:T(4,128)S(1)}, f32[4,1,1024]{2,0,1:T(4,128)S(1)}, u32[]{:S(2)}, u32[]{:S(2)}) collective-permute-start(f32[4,1,1024]{2,0,1:T(4,128)S(1)} %get-tuple-element.15), channel_id=1, source_target_pairs={{0,1},{1,2},{2,3},{4,5},{5,6},{6,7},{8,9},{9,10},{10,11},{12,13},{... | collective-permute-start | bytes 49160 | tf_op jit(solution)/shard_map/ppermute | solution.py:23
  14.8 1.9 %collective-permute-start.3 = (f32[4,1,1024]{2,0,1:T(4,128)S(1)}, f32[4,1,1024]{2,0,1:T(4,128)S(1)}, u32[]{:S(2)}, u32[]{:S(2)}) collective-permute-start(f32[4,1,1024]{2,0,1:T(4,128)S(1)} %get-tuple-element.16), channel_id=1, source_target_pairs={{1,0},{2,1},{3,2},{5,4},{6,5},{7,6},{9,8},{10,9},{11,10},{13,12},{... | collective-permute-start | bytes 49160 | tf_op jit(solution)/shard_map/ppermute | solution.py:25
  16.7 3.1 %collective-permute-done.3 = f32[4,1,1024]{2,0,1:T(4,128)S(1)} collective-permute-done((f32[4,1,1024]{2,0,1:T(4,128)S(1)}, f32[4,1,1024]{2,0,1:T(4,128)S(1)}, u32[]{:S(2)}, u32[]{:S(2)}) %collective-permute-start.3) | collective-permute-done | bytes 16416 | tf_op jit(solution)/shard_map/ppermute | solution.py:25
  19.8 0.1 fusion.45
  20.0 1.9 %collective-permute-start.4 = (f32[4,1,1024]{2,0,1:T(4,128)S(1)}, f32[4,1,1024]{2,0,1:T(4,128)S(1)}, u32[]{:S(2)}, u32[]{:S(2)}) collective-permute-start(f32[4,1,1024]{2,0,1:T(4,128)S(1)} %get-tuple-element.13), channel_id=1, source_target_pairs={{0,1},{1,2},{2,3},{4,5},{5,6},{6,7},{8,9},{9,10},{10,11},{12,13},{... | collective-permute-start | bytes 49160 | tf_op jit(solution)/shard_map/ppermute | solution.py:23
  21.9 2.4 %collective-permute-start.5 = (f32[4,1,1024]{2,0,1:T(4,128)S(1)}, f32[4,1,1024]{2,0,1:T(4,128)S(1)}, u32[]{:S(2)}, u32[]{:S(2)}) collective-permute-start(f32[4,1,1024]{2,0,1:T(4,128)S(1)} %get-tuple-element.14), channel_id=1, source_target_pairs={{1,0},{2,1},{3,2},{5,4},{6,5},{7,6},{9,8},{10,9},{11,10},{13,12},{... | collective-permute-start | bytes 49160 | tf_op jit(solution)/shard_map/ppermute | solution.py:25
  24.4 2.6 %collective-permute-done.5 = f32[4,1,1024]{2,0,1:T(4,128)S(1)} collective-permute-done((f32[4,1,1024]{2,0,1:T(4,128)S(1)}, f32[4,1,1024]{2,0,1:T(4,128)S(1)}, u32[]{:S(2)}, u32[]{:S(2)}) %collective-permute-start.5) | collective-permute-done | bytes 16416 | tf_op jit(solution)/shard_map/ppermute | solution.py:25
  27.0 0.1 fusion.32
  27.2 1.9 %collective-permute-start.6 = (f32[4,1,1024]{2,0,1:T(4,128)S(1)}, f32[4,1,1024]{2,0,1:T(4,128)S(1)}, u32[]{:S(2)}, u32[]{:S(2)}) collective-permute-start(f32[4,1,1024]{2,0,1:T(4,128)S(1)} %get-tuple-element.11), channel_id=1, source_target_pairs={{0,1},{1,2},{2,3},{4,5},{5,6},{6,7},{8,9},{9,10},{10,11},{12,13},{... | collective-permute-start | bytes 49160 | tf_op jit(solution)/shard_map/ppermute | solution.py:23
  29.1 2.4 %collective-permute-start.7 = (f32[4,1,1024]{2,0,1:T(4,128)S(1)}, f32[4,1,1024]{2,0,1:T(4,128)S(1)}, u32[]{:S(2)}, u32[]{:S(2)}) collective-permute-start(f32[4,1,1024]{2,0,1:T(4,128)S(1)} %get-tuple-element.12), channel_id=1, source_target_pairs={{1,0},{2,1},{3,2},{5,4},{6,5},{7,6},{9,8},{10,9},{11,10},{13,12},{... | collective-permute-start | bytes 49160 | tf_op jit(solution)/shard_map/ppermute | solution.py:25
  31.5 8.1 %scatter_custom_fusion = f32[5120]{0:T(1024)S(1)} fusion(s32[2048]{0:T(1024)S(1)} %bitcast.143, f32[2048]{0:T(1024)S(1)} %bitcast.144, f32[]{:T(128)} %constant.37.clone.1), kind=kCustom, calls=%fused_computation.134 | custom fusion | bytes 20484
  39.8 0.2 fusion.67
  39.9 0.8 copy.122
  40.7 2.6 %reshape.227 = bf16[8,2,1024]{2,1,0:T(2,128)(2,1)} reshape(bf16[1024,2,2,4]{3,2,1,0:T(2,128)(2,1)S(1)} %bitcast.128) | data formatting | bytes 65536
  43.3 5.6 %all-to-all-start = ((bf16[8,2,1024]{2,1,0:T(2,128)(2,1)}), bf16[8,2,1024]{2,1,0:T(2,128)(2,1)S(1)}, u32[]{:S(2)}, u32[]{:S(2)}) async-start(bf16[8,2,1024]{2,1,0:T(2,128)(2,1)} %reshape.227), calls=%async_computation | async-start | bytes 65536 | tf_op jit(solution)/shard_map/all_to_all | solution.py:143
  48.9 5.6 %all-to-all-done = bf16[8,2,1024]{2,1,0:T(2,128)(2,1)S(1)} async-done(((bf16[8,2,1024]{2,1,0:T(2,128)(2,1)}), bf16[8,2,1024]{2,1,0:T(2,128)(2,1)S(1)}, u32[]{:S(2)}, u32[]{:S(2)}) %all-to-all-start) | async-done | bytes 32800 | tf_op jit(solution)/shard_map/all_to_all | solution.py:143
  54.5 2.2 %reshape.228 = bf16[1024,2,2,4]{3,2,1,0:T(2,128)(2,1)S(1)} reshape(bf16[8,2,1024]{2,1,0:T(2,128)(2,1)S(1)} %all-to-all-done) | data formatting | bytes 65536
  56.7 1.3 %copy.123 = bf16[2,2,4,8,128]{4,3,2,1,0:T(8,128)(2,1)S(1)} copy(bf16[2,2,4,8,128]{2,1,0,4,3:T(2,128)(2,1)S(1)} %bitcast.129) | data formatting | bytes 65536 | tf_op jit(solution)/shard_map/all_to_all | solution.py:143
  58.1 0.1 copy.124
  58.2 0.9 gather_fusion
  59.1 0.1 convert_bitcast_fusion
  59.2 0.6 copy-done.4
  60.0 2.3 %collective-permute-start.8 = (f32[1,1,20,256]{3,2,1,0:T(8,128)S(1)}, f32[1,1,20,256]{3,2,1,0:T(8,128)S(1)}, u32[]{:S(2)}, u32[]{:S(2)}) collective-permute-start(f32[1,1,20,256]{3,2,1,0:T(8,128)S(1)} %bitcast.132), channel_id=1, source_target_pairs={{0,4},{4,8},{8,12},{12,16},{16,20},{20,24},{24,28},{1,5},{5,9},{9,... | collective-permute-start | bytes 61448 | tf_op jit(solution)/shard_map/ppermute | solution.py:23
  62.3 1.3 %collective-permute-start.9 = (f32[1,1,20,256]{3,2,1,0:T(8,128)S(1)}, f32[1,1,20,256]{3,2,1,0:T(8,128)S(1)}, u32[]{:S(2)}, u32[]{:S(2)}) collective-permute-start(f32[1,1,20,256]{3,2,1,0:T(8,128)S(1)} %bitcast.133), channel_id=1, source_target_pairs={{4,0},{8,4},{12,8},{16,12},{20,16},{24,20},{28,24},{5,1},{9,5},{13... | collective-permute-start | bytes 61448 | tf_op jit(solution)/shard_map/ppermute | solution.py:25
  63.7 3.1 %collective-permute-done.9 = f32[1,1,20,256]{3,2,1,0:T(8,128)S(1)} collective-permute-done((f32[1,1,20,256]{3,2,1,0:T(8,128)S(1)}, f32[1,1,20,256]{3,2,1,0:T(8,128)S(1)}, u32[]{:S(2)}, u32[]{:S(2)}) %collective-permute-start.9) | collective-permute-done | bytes 20512 | tf_op jit(solution)/shard_map/ppermute | solution.py:25
  66.9 5.7 %collective-permute-start.10 = (f32[1,3,20,256]{3,0,2,1:T(1,128)S(1)}, f32[1,3,20,256]{3,0,2,1:T(1,128)S(1)}, u32[]{:S(2)}, u32[]{:S(2)}) collective-permute-start(f32[1,3,20,256]{3,0,2,1:T(1,128)S(1)} %copy_dynamic-update-slice_fusion), channel_id=1, source_target_pairs={{0,1},{1,2},{2,3},{4,5},{5,6},{6,7},{8,9},{9,10},{10,11},{12,13},{... | collective-permute-start | bytes 184328 | tf_op jit(solution)/shard_map/ppermute | solution.py:23
  72.6 1.9 %collective-permute-start.11 = (f32[1,3,20,256]{3,0,2,1:T(1,128)S(1)}, f32[1,3,20,256]{3,0,2,1:T(1,128)S(1)}, u32[]{:S(2)}, u32[]{:S(2)}) collective-permute-start(f32[1,3,20,256]{3,0,2,1:T(1,128)S(1)} %copy_dynamic-update-slice_fusion), channel_id=1, source_target_pairs={{1,0},{2,1},{3,2},{5,4},{6,5},{7,6},{9,8},{10,9},{11,10},{13,12},{... | collective-permute-start | bytes 184328 | tf_op jit(solution)/shard_map/ppermute | solution.py:25
  74.6 3.5 %collective-permute-done.11 = f32[1,3,20,256]{3,0,2,1:T(1,128)S(1)} collective-permute-done((f32[1,3,20,256]{3,0,2,1:T(1,128)S(1)}, f32[1,3,20,256]{3,0,2,1:T(1,128)S(1)}, u32[]{:S(2)}, u32[]{:S(2)}) %collective-permute-start.11) | collective-permute-done | bytes 61472 | tf_op jit(solution)/shard_map/ppermute | solution.py:25
  78.4 1.3 %abs_reduce_fusion = (f32[4,16]{1,0:T(4,128)S(1)}, f32[4,16,16]{1,2,0:T(8,128)S(1)}) fusion(f32[16,1280]{1,0:T(8,128)S(1)} %slice_subtract_fusion, f32[4,1280]{1,0:T(4,128)S(1)} %multiply_multiply_fusion), kind=kOutput, calls=%fused_computation.104 | convolution fusion | flops 15812544 | bytes 106752 | tf_op jit(solution)/shard_map/rek,fk->ref/dot_general | solution.py:93
  79.7 0.1 reduce_max.9
  79.8 0.3 fusion.7
  80.1 0.3 fusion.97
  80.4 0.2 fusion.76
  80.6 0.2 fusion.6
  80.7 0.2 fusion.103
  80.9 0.2 fusion.102
  81.1 0.2 fusion.5
  81.3 0.2 fusion.105
  81.4 0.2 fusion.104
  81.6 0.2 fusion.4
  81.8 0.2 fusion.107
  81.9 0.2 fusion.106
  82.1 0.2 fusion.3
  82.3 0.2 fusion.109
  82.5 0.2 fusion.108
  82.6 0.2 fusion.72
  82.8 0.2 fusion.2
  83.0 0.2 convolution_divide_fusion
  83.2 0.2 convolution_bitcast_fusion.1
  83.3 0.2 fusion.110
  83.5 0.3 fusion.1
  83.9 8.8 %all_to_all.36 = bf16[16,2,4,128]{3,1,2,0:T(2,128)(2,1)S(1)} all-to-all(bf16[16,2,4,128]{3,1,2,0:T(2,128)(2,1)S(1)} %copy.112), channel_id=1, replica_groups=mesh['mem'=8,'lat'=4] {'mem'}, dimensions={0} | all-to-all | bytes 65536 | tf_op jit(solution)/shard_map/all_to_all | solution.py:168
  92.7 0.6 all_to_all.33
  (78 shorter events, 1.1 us)
Async XLA Ops:
  0.8 6.5 %copy-start = (f32[2,4,1024]{2,1,0:T(4,128)S(1)}, f32[2,4,1024]{2,1,0:T(4,128)}, u32[]{:S(2)}) copy-start(f32[2,4,1024]{2,1,0:T(4,128)} %param.9) | copy-start | bytes 98308
  0.8 6.5 %copy-start.1 = (s32[1,256]{1,0:T(1,128)S(1)}, s32[1,256]{1,0:T(1,128)}, u32[]{:S(2)}) copy-start(s32[1,256]{1,0:T(1,128)} %param.10) | copy-start | bytes 3076
  0.8 10.1 %collective-permute-start = (f32[4,1,1024]{2,0,1:T(4,128)S(1)}, f32[4,1,1024]{2,0,1:T(4,128)S(1)}, u32[]{:S(2)}, u32[]{:S(2)}) collective-permute-start(f32[4,1,1024]{2,0,1:T(4,128)S(1)} %get-tuple-element.17), channel_id=1, source_target_pairs={{0,1},{1,2},{2,3},{4,5},{5,6},{6,7},{8,9},{9,10},{10,11},{12,13},{... | collective-permute-start | bytes 49160 | tf_op jit(solution)/shard_map/ppermute | solution.py:23
  5.4 5.6 %collective-permute-start.1 = (f32[4,1,1024]{2,0,1:T(4,128)S(1)}, f32[4,1,1024]{2,0,1:T(4,128)S(1)}, u32[]{:S(2)}, u32[]{:S(2)}) collective-permute-start(f32[4,1,1024]{2,0,1:T(4,128)S(1)} %get-tuple-element.18), channel_id=1, source_target_pairs={{1,0},{2,1},{3,2},{5,4},{6,5},{7,6},{9,8},{10,9},{11,10},{13,12},{... | collective-permute-start | bytes 49160 | tf_op jit(solution)/shard_map/ppermute | solution.py:25
  7.3 0.7 copy-start.2
  8.1 0.7 copy-start.6
  8.7 0.7 copy-start.7
  9.5 0.7 copy-start.5
  10.2 0.7 copy-start.8
  11.1 5.6 %collective-permute-start.2 = (f32[4,1,1024]{2,0,1:T(4,128)S(1)}, f32[4,1,1024]{2,0,1:T(4,128)S(1)}, u32[]{:S(2)}, u32[]{:S(2)}) collective-permute-start(f32[4,1,1024]{2,0,1:T(4,128)S(1)} %get-tuple-element.15), channel_id=1, source_target_pairs={{0,1},{1,2},{2,3},{4,5},{5,6},{6,7},{8,9},{9,10},{10,11},{12,13},{... | collective-permute-start | bytes 49160 | tf_op jit(solution)/shard_map/ppermute | solution.py:23
  14.8 5.1 %collective-permute-start.3 = (f32[4,1,1024]{2,0,1:T(4,128)S(1)}, f32[4,1,1024]{2,0,1:T(4,128)S(1)}, u32[]{:S(2)}, u32[]{:S(2)}) collective-permute-start(f32[4,1,1024]{2,0,1:T(4,128)S(1)} %get-tuple-element.16), channel_id=1, source_target_pairs={{1,0},{2,1},{3,2},{5,4},{6,5},{7,6},{9,8},{10,9},{11,10},{13,12},{... | collective-permute-start | bytes 49160 | tf_op jit(solution)/shard_map/ppermute | solution.py:25
  20.0 4.4 %collective-permute-start.4 = (f32[4,1,1024]{2,0,1:T(4,128)S(1)}, f32[4,1,1024]{2,0,1:T(4,128)S(1)}, u32[]{:S(2)}, u32[]{:S(2)}) collective-permute-start(f32[4,1,1024]{2,0,1:T(4,128)S(1)} %get-tuple-element.13), channel_id=1, source_target_pairs={{0,1},{1,2},{2,3},{4,5},{5,6},{6,7},{8,9},{9,10},{10,11},{12,13},{... | collective-permute-start | bytes 49160 | tf_op jit(solution)/shard_map/ppermute | solution.py:23
  21.9 5.1 %collective-permute-start.5 = (f32[4,1,1024]{2,0,1:T(4,128)S(1)}, f32[4,1,1024]{2,0,1:T(4,128)S(1)}, u32[]{:S(2)}, u32[]{:S(2)}) collective-permute-start(f32[4,1,1024]{2,0,1:T(4,128)S(1)} %get-tuple-element.14), channel_id=1, source_target_pairs={{1,0},{2,1},{3,2},{5,4},{6,5},{7,6},{9,8},{10,9},{11,10},{13,12},{... | collective-permute-start | bytes 49160 | tf_op jit(solution)/shard_map/ppermute | solution.py:25
  27.2 12.6 %collective-permute-start.6 = (f32[4,1,1024]{2,0,1:T(4,128)S(1)}, f32[4,1,1024]{2,0,1:T(4,128)S(1)}, u32[]{:S(2)}, u32[]{:S(2)}) collective-permute-start(f32[4,1,1024]{2,0,1:T(4,128)S(1)} %get-tuple-element.11), channel_id=1, source_target_pairs={{0,1},{1,2},{2,3},{4,5},{5,6},{6,7},{8,9},{9,10},{10,11},{12,13},{... | collective-permute-start | bytes 49160 | tf_op jit(solution)/shard_map/ppermute | solution.py:23
  29.1 10.7 %collective-permute-start.7 = (f32[4,1,1024]{2,0,1:T(4,128)S(1)}, f32[4,1,1024]{2,0,1:T(4,128)S(1)}, u32[]{:S(2)}, u32[]{:S(2)}) collective-permute-start(f32[4,1,1024]{2,0,1:T(4,128)S(1)} %get-tuple-element.12), channel_id=1, source_target_pairs={{1,0},{2,1},{3,2},{5,4},{6,5},{7,6},{9,8},{10,9},{11,10},{13,12},{... | collective-permute-start | bytes 49160 | tf_op jit(solution)/shard_map/ppermute | solution.py:25
  43.3 11.2 %all-to-all-start = ((bf16[8,2,1024]{2,1,0:T(2,128)(2,1)}), bf16[8,2,1024]{2,1,0:T(2,128)(2,1)S(1)}, u32[]{:S(2)}, u32[]{:S(2)}) async-start(bf16[8,2,1024]{2,1,0:T(2,128)(2,1)} %reshape.227), calls=%async_computation | async-start | bytes 65536 | tf_op jit(solution)/shard_map/all_to_all | solution.py:143
  59.2 0.7 copy-start.4
  59.2 0.7 copy-start.3
  60.0 3.7 %collective-permute-start.8 = (f32[1,1,20,256]{3,2,1,0:T(8,128)S(1)}, f32[1,1,20,256]{3,2,1,0:T(8,128)S(1)}, u32[]{:S(2)}, u32[]{:S(2)}) collective-permute-start(f32[1,1,20,256]{3,2,1,0:T(8,128)S(1)} %bitcast.132), channel_id=1, source_target_pairs={{0,4},{4,8},{8,12},{12,16},{16,20},{20,24},{24,28},{1,5},{5,9},{9,... | collective-permute-start | bytes 61448 | tf_op jit(solution)/shard_map/ppermute | solution.py:23
  62.3 4.6 %collective-permute-start.9 = (f32[1,1,20,256]{3,2,1,0:T(8,128)S(1)}, f32[1,1,20,256]{3,2,1,0:T(8,128)S(1)}, u32[]{:S(2)}, u32[]{:S(2)}) collective-permute-start(f32[1,1,20,256]{3,2,1,0:T(8,128)S(1)} %bitcast.133), channel_id=1, source_target_pairs={{4,0},{8,4},{12,8},{16,12},{20,16},{24,20},{28,24},{5,1},{9,5},{13... | collective-permute-start | bytes 61448 | tf_op jit(solution)/shard_map/ppermute | solution.py:25
  66.9 7.7 %collective-permute-start.10 = (f32[1,3,20,256]{3,0,2,1:T(1,128)S(1)}, f32[1,3,20,256]{3,0,2,1:T(1,128)S(1)}, u32[]{:S(2)}, u32[]{:S(2)}) collective-permute-start(f32[1,3,20,256]{3,0,2,1:T(1,128)S(1)} %copy_dynamic-update-slice_fusion), channel_id=1, source_target_pairs={{0,1},{1,2},{2,3},{4,5},{5,6},{6,7},{8,9},{9,10},{10,11},{12,13},{... | collective-permute-start | bytes 184328 | tf_op jit(solution)/shard_map/ppermute | solution.py:23
  72.6 5.5 %collective-permute-start.11 = (f32[1,3,20,256]{3,0,2,1:T(1,128)S(1)}, f32[1,3,20,256]{3,0,2,1:T(1,128)S(1)}, u32[]{:S(2)}, u32[]{:S(2)}) collective-permute-start(f32[1,3,20,256]{3,0,2,1:T(1,128)S(1)} %copy_dynamic-update-slice_fusion), channel_id=1, source_target_pairs={{1,0},{2,1},{3,2},{5,4},{6,5},{7,6},{9,8},{10,9},{11,10},{13,12},{... | collective-permute-start | bytes 184328 | tf_op jit(solution)/shard_map/ppermute | solution.py:25
where the time goes:
time: 94 us; the launch traced here: 93.3 us
  starting transfers between devices  37.4 us (40%)
  local copies, waits for them, and re-layouts  21 us (22%)
  waiting for transfers between devices  18.1 us (19%)
  blocking collectives  8.78 us (9%)
  matrix products  5.2 us (6%)
  other arithmetic  2.15 us (2%)
    ppermute x6, starting transfers between devices, with_halo(): lax.ppermute(tail, axis, [(i, (i + 1) % count) for i in range(ends)])  20 us
    unnamed x28, local copies, waits for them, and re-layouts  16.8 us
    ppermute x6, waiting for transfers between devices, with_halo(): lax.ppermute(head, axis, [((i + 1) % count, i) for i in range(ends)])  12.4 us
    ppermute x6, starting transfers between devices, with_halo(): lax.ppermute(head, axis, [((i + 1) % count, i) for i in range(ends)])  11.8 us
    all_to_all x1, blocking collectives, on_device(): lax.all_to_all(updated, 'mem', split_axis=0, concat_axis=3, tiled=True)  8.78 us
    all_to_all x1, waiting for transfers between devices, on_device(): lax.all_to_all(predict_advance, 'mem', split_axis=3, concat_axis=0, tiled...  5.62 us
    all_to_all x1, starting transfers between devices, on_device(): lax.all_to_all(predict_advance, 'mem', split_axis=3, concat_axis=0, tiled...  5.55 us
  transfers between devices with their start and end apart: 13, of which 5 were waited for; matrix products, arithmetic and copies ran while one was open for 9% of the time, Pallas kernels for 0%

commit v1 on v0

--- a/solution.py
+++ b/solution.py
@@ -10,6 +10,17 @@
 LOC_COLS = 64
 KAPPA = (0.025, 0.0125)
 HIGHEST = lax.Precision.HIGHEST
+
+
+def test_the_wires(patch, pos_dim, a0):
+    parts_out, local_now = (patch.shape[:pos_dim], patch.shape[pos_dim + 1 :])
+    return jnp.moveaxis(patch.reshape(*parts_out, a0, -1, *local_now), pos_dim, 0)
+
+
+def obtain_joints(tile_in, array_dim):
+    new = list(tile_in.shape[1:])
+    new[array_dim] *= tile_in.shape[0]
+    return jnp.moveaxis(tile_in, 0, array_dim).reshape(new)
 
 
 def with_halo(cells, sides, width):
@@ -140,7 +151,14 @@
         ],
         axis=0,
     )
-    mesh_patches = lax.all_to_all(predict_advance, "mem", split_axis=3, concat_axis=0, tiled=True)
+    all_values, y2 = (lax.psum(1, "mem"), lax.axis_index("mem"))
+    opened = test_the_wires(predict_advance, 3, all_values)
+    copies = [opened[y2]]
+    for p in [*range(1, all_values)]:
+        back = opened[y2 ^ p]
+        copies.append(lax.ppermute(back, "mem", [(at, at ^ p) for at in range(all_values)]))
+    opened = jnp.stack(copies, 0)[y2 ^ jnp.arange(all_values)]
+    mesh_patches = obtain_joints(opened, 0)
     sample_realizations = mesh_patches.shape[0]
     own_obs = jnp.take(mesh_patches[:, 0].reshape(sample_realizations, -1), cells, axis=1).astype(
         jnp.float32

time: 94 us -> 90.1 us (0.959)
  the two profiles are of different devices: /device:TPU:1 before, /device:TPU:2 now
where the time goes in v1:
time: 90.1 us; the launch traced here: 89.4 us
  starting transfers between devices  42.5 us (47%)
  local copies, waits for them, and re-layouts  14.4 us (16%)
  waiting for transfers between devices  13.4 us (15%)
  blocking collectives  10.9 us (12%)
  matrix products  5.19 us (6%)
  other arithmetic  2.24 us (2%)
    ppermute x6, starting transfers between devices, with_halo(): lax.ppermute(head, axis, [((i + 1) % count, i) for i in range(ends)])  16.1 us
    ppermute x6, starting transfers between devices, with_halo(): lax.ppermute(tail, axis, [(i, (i + 1) % count) for i in range(ends)])  15.1 us
    unnamed x42, local copies, waits for them, and re-layouts  11.5 us
    ppermute x7, starting transfers between devices, on_device(): lax.ppermute(back, 'mem', [(at, at ^ p) for at in range(all_values)])  11.3 us
    all_to_all x1, blocking collectives, on_device(): lax.all_to_all(updated, 'mem', split_axis=0, concat_axis=3, tiled=True)  10.9 us
    ppermute x7, waiting for transfers between devices, on_device(): lax.ppermute(back, 'mem', [(at, at ^ p) for at in range(all_values)])  6.07 us
    ppermute x6, waiting for transfers between devices, with_halo(): lax.ppermute(tail, axis, [(i, (i + 1) % count) for i in range(ends)])  4.52 us
    ppermute x6, waiting for transfers between devices, with_halo(): lax.ppermute(head, axis, [((i + 1) % count, i) for i in range(ends)])  2.8 us
  transfers between devices with their start and end apart: 19, of which 7 were waited for; matrix products, arithmetic and copies ran while one was open for 10% of the time, Pallas kernels for 0%

profile of v1, /device:TPU:2, one launch (start us, length us, event | category | flops | bytes accessed | tf_op | source)
XLA Modules:
  0.0 89.4 jit_solution(1149950566332972753)
XLA Ops:
  0.0 0.8 bitcast_convert_fusion
  0.8 1.9 %collective-permute-start.1 = (f32[4,1,1024]{2,1,0:T(1,128)S(1)}, f32[4,1,1024]{2,1,0:T(1,128)S(1)}, u32[]{:S(2)}, u32[]{:S(2)}) collective-permute-start(f32[4,1,1024]{2,1,0:T(1,128)S(1)} %get-tuple-element.17), channel_id=1, source_target_pairs={{1,0},{2,1},{3,2},{5,4},{6,5},{7,6},{9,8},{10,9},{11,10},{13,12},{... | collective-permute-start | bytes 49160 | tf_op jit(solution)/shard_map/ppermute | solution.py:36
  2.7 2.4 %collective-permute-start = (f32[4,1,1024]{2,1,0:T(1,128)S(1)}, f32[4,1,1024]{2,1,0:T(1,128)S(1)}, u32[]{:S(2)}, u32[]{:S(2)}) collective-permute-start(f32[4,1,1024]{2,1,0:T(1,128)S(1)} %get-tuple-element.18), channel_id=1, source_target_pairs={{0,1},{1,2},{2,3},{4,5},{5,6},{6,7},{8,9},{9,10},{10,11},{12,13},{... | collective-permute-start | bytes 49160 | tf_op jit(solution)/shard_map/ppermute | solution.py:34
  5.3 0.6 copy-done.3
  5.9 0.6 copy-done.7
  6.8 0.6 copy-done.6
  7.6 0.6 copy-done.9
  8.3 0.2 fusion.20
  8.5 1.9 %collective-permute-start.2 = (f32[4,1,1024]{2,1,0:T(1,128)S(1)}, f32[4,1,1024]{2,1,0:T(1,128)S(1)}, u32[]{:S(2)}, u32[]{:S(2)}) collective-permute-start(f32[4,1,1024]{2,1,0:T(1,128)S(1)} %get-tuple-element.15), channel_id=1, source_target_pairs={{0,1},{1,2},{2,3},{4,5},{5,6},{6,7},{8,9},{9,10},{10,11},{12,13},{... | collective-permute-start | bytes 49160 | tf_op jit(solution)/shard_map/ppermute | solution.py:34
  10.4 3.6 %collective-permute-start.3 = (f32[4,1,1024]{2,1,0:T(1,128)S(1)}, f32[4,1,1024]{2,1,0:T(1,128)S(1)}, u32[]{:S(2)}, u32[]{:S(2)}) collective-permute-start(f32[4,1,1024]{2,1,0:T(1,128)S(1)} %get-tuple-element.16), channel_id=1, source_target_pairs={{1,0},{2,1},{3,2},{5,4},{6,5},{7,6},{9,8},{10,9},{11,10},{13,12},{... | collective-permute-start | bytes 49160 | tf_op jit(solution)/shard_map/ppermute | solution.py:36
  14.1 1.4 %collective-permute-done.3 = f32[4,1,1024]{2,1,0:T(1,128)S(1)} collective-permute-done((f32[4,1,1024]{2,1,0:T(1,128)S(1)}, f32[4,1,1024]{2,1,0:T(1,128)S(1)}, u32[]{:S(2)}, u32[]{:S(2)}) %collective-permute-start.3) | collective-permute-done | bytes 16416 | tf_op jit(solution)/shard_map/ppermute | solution.py:36
  15.5 0.2 fusion.55
  15.7 1.9 %collective-permute-start.4 = (f32[4,1,1024]{2,1,0:T(1,128)S(1)}, f32[4,1,1024]{2,1,0:T(1,128)S(1)}, u32[]{:S(2)}, u32[]{:S(2)}) collective-permute-start(f32[4,1,1024]{2,1,0:T(1,128)S(1)} %get-tuple-element.13), channel_id=1, source_target_pairs={{0,1},{1,2},{2,3},{4,5},{5,6},{6,7},{8,9},{9,10},{10,11},{12,13},{... | collective-permute-start | bytes 49160 | tf_op jit(solution)/shard_map/ppermute | solution.py:34
  17.6 3.6 %collective-permute-start.5 = (f32[4,1,1024]{2,1,0:T(1,128)S(1)}, f32[4,1,1024]{2,1,0:T(1,128)S(1)}, u32[]{:S(2)}, u32[]{:S(2)}) collective-permute-start(f32[4,1,1024]{2,1,0:T(1,128)S(1)} %get-tuple-element.14), channel_id=1, source_target_pairs={{1,0},{2,1},{3,2},{5,4},{6,5},{7,6},{9,8},{10,9},{11,10},{13,12},{... | collective-permute-start | bytes 49160 | tf_op jit(solution)/shard_map/ppermute | solution.py:36
  21.3 1.4 %collective-permute-done.5 = f32[4,1,1024]{2,1,0:T(1,128)S(1)} collective-permute-done((f32[4,1,1024]{2,1,0:T(1,128)S(1)}, f32[4,1,1024]{2,1,0:T(1,128)S(1)}, u32[]{:S(2)}, u32[]{:S(2)}) %collective-permute-start.5) | collective-permute-done | bytes 16416 | tf_op jit(solution)/shard_map/ppermute | solution.py:36
  22.7 0.2 fusion.42
  22.9 1.9 %collective-permute-start.6 = (f32[4,1,1024]{2,1,0:T(1,128)S(1)}, f32[4,1,1024]{2,1,0:T(1,128)S(1)}, u32[]{:S(2)}, u32[]{:S(2)}) collective-permute-start(f32[4,1,1024]{2,1,0:T(1,128)S(1)} %get-tuple-element.11), channel_id=1, source_target_pairs={{0,1},{1,2},{2,3},{4,5},{5,6},{6,7},{8,9},{9,10},{10,11},{12,13},{... | collective-permute-start | bytes 49160 | tf_op jit(solution)/shard_map/ppermute | solution.py:34
  24.8 3.6 %collective-permute-start.7 = (f32[4,1,1024]{2,1,0:T(1,128)S(1)}, f32[4,1,1024]{2,1,0:T(1,128)S(1)}, u32[]{:S(2)}, u32[]{:S(2)}) collective-permute-start(f32[4,1,1024]{2,1,0:T(1,128)S(1)} %get-tuple-element.12), channel_id=1, source_target_pairs={{1,0},{2,1},{3,2},{5,4},{6,5},{7,6},{9,8},{10,9},{11,10},{13,12},{... | collective-permute-start | bytes 49160 | tf_op jit(solution)/shard_map/ppermute | solution.py:36
  28.5 8.1 %scatter_custom_fusion = f32[5120]{0:T(1024)S(1)} fusion(s32[2048]{0:T(1024)S(1)} %bitcast.175, f32[2048]{0:T(1024)S(1)} %bitcast.176, f32[]{:T(128)} %constant.34.clone.1), kind=kCustom, calls=%fused_computation.146 | custom fusion | bytes 20484
  36.8 0.2 fusion.64
  37.1 1.6 %collective-permute-start.8 = (bf16[2,2,4,128]{3,2,1,0:T(4,128)(2,1)S(1)}, bf16[2,2,4,128]{3,2,1,0:T(4,128)(2,1)S(1)}, u32[]{:S(2)}, u32[]{:S(2)}) collective-permute-start(bf16[2,2,4,128]{3,2,1,0:T(4,128)(2,1)S(1)} %bitcast.183), channel_id=1, source_target_pairs={{0,4},{4,0},{8,12},{12,8},{16,20},{20,16},{24,28},{28,24},{1,5},{5... | collective-permute-start | bytes 12296 | tf_op jit(solution)/shard_map/ppermute | solution.py:159
  38.7 1.6 %collective-permute-start.9 = (bf16[2,2,4,128]{3,2,1,0:T(4,128)(2,1)S(1)}, bf16[2,2,4,128]{3,2,1,0:T(4,128)(2,1)S(1)}, u32[]{:S(2)}, u32[]{:S(2)}) collective-permute-start(bf16[2,2,4,128]{3,2,1,0:T(4,128)(2,1)S(1)} %bitcast.182), channel_id=1, source_target_pairs={{0,8},{4,12},{8,0},{12,4},{16,24},{20,28},{24,16},{28,20},{1,9},{5... | collective-permute-start | bytes 12296 | tf_op jit(solution)/shard_map/ppermute | solution.py:159
  40.3 0.4 collective-permute-start.10
  40.7 2.6 %collective-permute-start.11 = (bf16[2,2,4,128]{3,2,1,0:T(4,128)(2,1)S(1)}, bf16[2,2,4,128]{3,2,1,0:T(4,128)(2,1)S(1)}, u32[]{:S(2)}, u32[]{:S(2)}) collective-permute-start(bf16[2,2,4,128]{3,2,1,0:T(4,128)(2,1)S(1)} %bitcast.178), channel_id=1, source_target_pairs={{0,16},{4,20},{8,24},{12,28},{16,0},{20,4},{24,8},{28,12},{1,17},{... | collective-permute-start | bytes 12296 | tf_op jit(solution)/shard_map/ppermute | solution.py:159
  43.2 1.3 %collective-permute-start.12 = (bf16[2,2,4,128]{3,2,1,0:T(4,128)(2,1)S(1)}, bf16[2,2,4,128]{3,2,1,0:T(4,128)(2,1)S(1)}, u32[]{:S(2)}, u32[]{:S(2)}) collective-permute-start(bf16[2,2,4,128]{3,2,1,0:T(4,128)(2,1)S(1)} %bitcast.177), channel_id=1, source_target_pairs={{0,20},{4,16},{8,28},{12,24},{16,4},{20,0},{24,12},{28,8},{1,21},{... | collective-permute-start | bytes 12296 | tf_op jit(solution)/shard_map/ppermute | solution.py:159
  44.6 3.7 %collective-permute-start.13 = (bf16[2,2,4,128]{3,2,1,0:T(4,128)(2,1)S(1)}, bf16[2,2,4,128]{3,2,1,0:T(4,128)(2,1)S(1)}, u32[]{:S(2)}, u32[]{:S(2)}) collective-permute-start(bf16[2,2,4,128]{3,2,1,0:T(4,128)(2,1)S(1)} %bitcast.181), channel_id=1, source_target_pairs={{0,24},{4,28},{8,16},{12,20},{16,8},{20,12},{24,0},{28,4},{1,25},{... | collective-permute-start | bytes 12296 | tf_op jit(solution)/shard_map/ppermute | solution.py:159
  48.3 0.2 collective-permute-start.14
  48.7 1.4 %collective-permute-done.13 = bf16[2,2,4,128]{3,2,1,0:T(4,128)(2,1)S(1)} collective-permute-done((bf16[2,2,4,128]{3,2,1,0:T(4,128)(2,1)S(1)}, bf16[2,2,4,128]{3,2,1,0:T(4,128)(2,1)S(1)}, u32[]{:S(2)}, u32[]{:S(2)}) %collective-permute-start.13) | collective-permute-done | bytes 4128 | tf_op jit(solution)/shard_map/ppermute | solution.py:159
  50.1 4.6 %collective-permute-done.14 = bf16[2,2,4,128]{3,2,1,0:T(4,128)(2,1)S(1)} collective-permute-done((bf16[2,2,4,128]{3,2,1,0:T(4,128)(2,1)S(1)}, bf16[2,2,4,128]{3,2,1,0:T(4,128)(2,1)S(1)}, u32[]{:S(2)}, u32[]{:S(2)}) %collective-permute-start.14) | collective-permute-done | bytes 4128 | tf_op jit(solution)/shard_map/ppermute | solution.py:159
  54.6 0.6 gather_fusion
  55.3 0.1 copy.105
  55.4 0.9 gather_fusion.1
  56.5 0.6 copy-done.5
  57.2 1.3 %collective-permute-start.16 = (f32[1,1,20,256]{3,2,1,0:T(8,128)S(1)}, f32[1,1,20,256]{3,2,1,0:T(8,128)S(1)}, u32[]{:S(2)}, u32[]{:S(2)}) collective-permute-start(f32[1,1,20,256]{3,2,1,0:T(8,128)S(1)} %bitcast.164), channel_id=1, source_target_pairs={{4,0},{8,4},{12,8},{16,12},{20,16},{24,20},{28,24},{5,1},{9,5},{13... | collective-permute-start | bytes 61448 | tf_op jit(solution)/shard_map/ppermute | solution.py:36
  58.5 4.5 %collective-permute-start.15 = (f32[1,1,20,256]{3,2,1,0:T(8,128)S(1)}, f32[1,1,20,256]{3,2,1,0:T(8,128)S(1)}, u32[]{:S(2)}, u32[]{:S(2)}) collective-permute-start(f32[1,1,20,256]{3,2,1,0:T(8,128)S(1)} %bitcast.165), channel_id=1, source_target_pairs={{0,4},{4,8},{8,12},{12,16},{16,20},{20,24},{24,28},{1,5},{5,9},{9,... | collective-permute-start | bytes 61448 | tf_op jit(solution)/shard_map/ppermute | solution.py:34
  63.1 1.5 %collective-permute-done.15 = f32[1,1,20,256]{3,2,1,0:T(8,128)S(1)} collective-permute-done((f32[1,1,20,256]{3,2,1,0:T(8,128)S(1)}, f32[1,1,20,256]{3,2,1,0:T(8,128)S(1)}, u32[]{:S(2)}, u32[]{:S(2)}) %collective-permute-start.15) | collective-permute-done | bytes 20512 | tf_op jit(solution)/shard_map/ppermute | solution.py:34
  64.6 1.9 %collective-permute-start.18 = (f32[1,3,20,256]{3,0,2,1:T(1,128)S(1)}, f32[1,3,20,256]{3,0,2,1:T(1,128)S(1)}, u32[]{:S(2)}, u32[]{:S(2)}) collective-permute-start(f32[1,3,20,256]{3,0,2,1:T(1,128)S(1)} %constant_dynamic-update-slice_fusion.8), channel_id=1, source_target_pairs={{1,0},{2,1},{3,2},{5,4},{6,5},{7,6},{9,8},{10,9},{11,10},{13,12},{... | collective-permute-start | bytes 184328 | tf_op jit(solution)/shard_map/ppermute | solution.py:36
  66.6 2.4 %collective-permute-start.17 = (f32[1,3,20,256]{3,0,2,1:T(1,128)S(1)}, f32[1,3,20,256]{3,0,2,1:T(1,128)S(1)}, u32[]{:S(2)}, u32[]{:S(2)}) collective-permute-start(f32[1,3,20,256]{3,0,2,1:T(1,128)S(1)} %constant_dynamic-update-slice_fusion.8), channel_id=1, source_target_pairs={{0,1},{1,2},{2,3},{4,5},{5,6},{6,7},{8,9},{9,10},{10,11},{12,13},{... | collective-permute-start | bytes 184328 | tf_op jit(solution)/shard_map/ppermute | solution.py:34
  69.1 3.0 %collective-permute-done.17 = f32[1,3,20,256]{3,0,2,1:T(1,128)S(1)} collective-permute-done((f32[1,3,20,256]{3,0,2,1:T(1,128)S(1)}, f32[1,3,20,256]{3,0,2,1:T(1,128)S(1)}, u32[]{:S(2)}, u32[]{:S(2)}) %collective-permute-start.17) | collective-permute-done | bytes 61472 | tf_op jit(solution)/shard_map/ppermute | solution.py:34
  72.4 1.3 %abs_reduce_fusion = (f32[4,16]{1,0:T(4,128)S(1)}, f32[4,16,16]{1,2,0:T(8,128)S(1)}) fusion(f32[16,1280]{1,0:T(8,128)S(1)} %slice_subtract_fusion, f32[4,1280]{1,0:T(4,128)S(1)} %multiply_multiply_fusion), kind=kOutput, calls=%fused_computation.124 | convolution fusion | flops 15812544 | bytes 106752 | tf_op jit(solution)/shard_map/rek,fk->ref/dot_general | solution.py:104
  73.6 0.1 reduce_max.9
  73.8 0.3 fusion.7
  74.0 0.3 fusion.95
  74.4 0.2 fusion.73
  74.5 0.2 fusion.6
  74.7 0.2 fusion.101
  74.9 0.2 fusion.100
  75.0 0.2 fusion.5
  75.2 0.2 fusion.103
  75.4 0.2 fusion.102
  75.6 0.2 fusion.4
  75.7 0.2 fusion.105
  75.9 0.2 fusion.104
  76.1 0.2 fusion.3
  76.2 0.2 fusion.106
  76.4 0.2 fusion.107
  76.6 0.2 fusion.69
  76.8 0.2 fusion.2
  77.0 0.2 convolution_divide_fusion
  77.1 0.2 convolution_bitcast_fusion.1
  77.3 0.2 fusion.108
  77.5 0.3 fusion.1
  77.9 10.9 %all_to_all.18 = bf16[16,2,4,128]{3,1,2,0:T(2,128)(2,1)S(1)} all-to-all(bf16[16,2,4,128]{3,1,2,0:T(2,128)(2,1)S(1)} %copy.96), channel_id=1, replica_groups=mesh['mem'=8,'lat'=4] {'mem'}, dimensions={0} | all-to-all | bytes 65536 | tf_op jit(solution)/shard_map/all_to_all | solution.py:186
  88.8 0.6 all_to_all.16
  (107 shorter events, 1.8 us)
Async XLA Ops:
  0.8 4.4 %copy-start.2 = (s32[1,256]{1,0:T(1,128)S(1)}, s32[1,256]{1,0:T(1,128)}, u32[]{:S(2)}) copy-start(s32[1,256]{1,0:T(1,128)} %param.10) | copy-start | bytes 3076
  0.8 7.4 %collective-permute-start.1 = (f32[4,1,1024]{2,1,0:T(1,128)S(1)}, f32[4,1,1024]{2,1,0:T(1,128)S(1)}, u32[]{:S(2)}, u32[]{:S(2)}) collective-permute-start(f32[4,1,1024]{2,1,0:T(1,128)S(1)} %get-tuple-element.17), channel_id=1, source_target_pairs={{1,0},{2,1},{3,2},{5,4},{6,5},{7,6},{9,8},{10,9},{11,10},{13,12},{... | collective-permute-start | bytes 49160 | tf_op jit(solution)/shard_map/ppermute | solution.py:36
  2.7 5.5 %collective-permute-start = (f32[4,1,1024]{2,1,0:T(1,128)S(1)}, f32[4,1,1024]{2,1,0:T(1,128)S(1)}, u32[]{:S(2)}, u32[]{:S(2)}) collective-permute-start(f32[4,1,1024]{2,1,0:T(1,128)S(1)} %get-tuple-element.18), channel_id=1, source_target_pairs={{0,1},{1,2},{2,3},{4,5},{5,6},{6,7},{8,9},{9,10},{10,11},{12,13},{... | collective-permute-start | bytes 49160 | tf_op jit(solution)/shard_map/ppermute | solution.py:34
  5.2 0.7 copy-start.3
  5.9 0.7 copy-start.7
  5.9 0.8 copy-start.8
  5.9 1.6 %copy-start.1 = (f32[2,4,1024]{2,1,0:T(4,128)S(1)}, f32[2,4,1024]{2,1,0:T(4,128)}, u32[]{:S(2)}) copy-start(f32[2,4,1024]{2,1,0:T(4,128)} %param.9) | copy-start | bytes 98308
  6.8 0.7 copy-start.6
  7.5 0.7 copy-start.9
  7.5 0.8 copy-start
  8.5 5.6 %collective-permute-start.2 = (f32[4,1,1024]{2,1,0:T(1,128)S(1)}, f32[4,1,1024]{2,1,0:T(1,128)S(1)}, u32[]{:S(2)}, u32[]{:S(2)}) collective-permute-start(f32[4,1,1024]{2,1,0:T(1,128)S(1)} %get-tuple-element.15), channel_id=1, source_target_pairs={{0,1},{1,2},{2,3},{4,5},{5,6},{6,7},{8,9},{9,10},{10,11},{12,13},{... | collective-permute-start | bytes 49160 | tf_op jit(solution)/shard_map/ppermute | solution.py:34
  10.4 5.1 %collective-permute-start.3 = (f32[4,1,1024]{2,1,0:T(1,128)S(1)}, f32[4,1,1024]{2,1,0:T(1,128)S(1)}, u32[]{:S(2)}, u32[]{:S(2)}) collective-permute-start(f32[4,1,1024]{2,1,0:T(1,128)S(1)} %get-tuple-element.16), channel_id=1, source_target_pairs={{1,0},{2,1},{3,2},{5,4},{6,5},{7,6},{9,8},{10,9},{11,10},{13,12},{... | collective-permute-start | bytes 49160 | tf_op jit(solution)/shard_map/ppermute | solution.py:36
  15.7 5.6 %collective-permute-start.4 = (f32[4,1,1024]{2,1,0:T(1,128)S(1)}, f32[4,1,1024]{2,1,0:T(1,128)S(1)}, u32[]{:S(2)}, u32[]{:S(2)}) collective-permute-start(f32[4,1,1024]{2,1,0:T(1,128)S(1)} %get-tuple-element.13), channel_id=1, source_target_pairs={{0,1},{1,2},{2,3},{4,5},{5,6},{6,7},{8,9},{9,10},{10,11},{12,13},{... | collective-permute-start | bytes 49160 | tf_op jit(solution)/shard_map/ppermute | solution.py:34
  17.6 5.1 %collective-permute-start.5 = (f32[4,1,1024]{2,1,0:T(1,128)S(1)}, f32[4,1,1024]{2,1,0:T(1,128)S(1)}, u32[]{:S(2)}, u32[]{:S(2)}) collective-permute-start(f32[4,1,1024]{2,1,0:T(1,128)S(1)} %get-tuple-element.14), channel_id=1, source_target_pairs={{1,0},{2,1},{3,2},{5,4},{6,5},{7,6},{9,8},{10,9},{11,10},{13,12},{... | collective-permute-start | bytes 49160 | tf_op jit(solution)/shard_map/ppermute | solution.py:36
  22.9 13.9 %collective-permute-start.6 = (f32[4,1,1024]{2,1,0:T(1,128)S(1)}, f32[4,1,1024]{2,1,0:T(1,128)S(1)}, u32[]{:S(2)}, u32[]{:S(2)}) collective-permute-start(f32[4,1,1024]{2,1,0:T(1,128)S(1)} %get-tuple-element.11), channel_id=1, source_target_pairs={{0,1},{1,2},{2,3},{4,5},{5,6},{6,7},{8,9},{9,10},{10,11},{12,13},{... | collective-permute-start | bytes 49160 | tf_op jit(solution)/shard_map/ppermute | solution.py:34
  24.8 12.0 %collective-permute-start.7 = (f32[4,1,1024]{2,1,0:T(1,128)S(1)}, f32[4,1,1024]{2,1,0:T(1,128)S(1)}, u32[]{:S(2)}, u32[]{:S(2)}) collective-permute-start(f32[4,1,1024]{2,1,0:T(1,128)S(1)} %get-tuple-element.12), channel_id=1, source_target_pairs={{1,0},{2,1},{3,2},{5,4},{6,5},{7,6},{9,8},{10,9},{11,10},{13,12},{... | collective-permute-start | bytes 49160 | tf_op jit(solution)/shard_map/ppermute | solution.py:36
  37.1 7.5 %collective-permute-start.8 = (bf16[2,2,4,128]{3,2,1,0:T(4,128)(2,1)S(1)}, bf16[2,2,4,128]{3,2,1,0:T(4,128)(2,1)S(1)}, u32[]{:S(2)}, u32[]{:S(2)}) collective-permute-start(bf16[2,2,4,128]{3,2,1,0:T(4,128)(2,1)S(1)} %bitcast.183), channel_id=1, source_target_pairs={{0,4},{4,0},{8,12},{12,8},{16,20},{20,16},{24,28},{28,24},{1,5},{5... | collective-permute-start | bytes 12296 | tf_op jit(solution)/shard_map/ppermute | solution.py:159
  38.7 9.6 %collective-permute-start.9 = (bf16[2,2,4,128]{3,2,1,0:T(4,128)(2,1)S(1)}, bf16[2,2,4,128]{3,2,1,0:T(4,128)(2,1)S(1)}, u32[]{:S(2)}, u32[]{:S(2)}) collective-permute-start(bf16[2,2,4,128]{3,2,1,0:T(4,128)(2,1)S(1)} %bitcast.182), channel_id=1, source_target_pairs={{0,8},{4,12},{8,0},{12,4},{16,24},{20,28},{24,16},{28,20},{1,9},{5... | collective-permute-start | bytes 12296 | tf_op jit(solution)/shard_map/ppermute | solution.py:159
  40.3 8.2 %collective-permute-start.10 = (bf16[2,2,4,128]{3,2,1,0:T(4,128)(2,1)S(1)}, bf16[2,2,4,128]{3,2,1,0:T(4,128)(2,1)S(1)}, u32[]{:S(2)}, u32[]{:S(2)}) collective-permute-start(bf16[2,2,4,128]{3,2,1,0:T(4,128)(2,1)S(1)} %bitcast.179), channel_id=1, source_target_pairs={{0,12},{4,8},{8,4},{12,0},{16,28},{20,24},{24,20},{28,16},{1,13},{... | collective-permute-start | bytes 12296 | tf_op jit(solution)/shard_map/ppermute | solution.py:159
  40.7 7.9 %collective-permute-start.11 = (bf16[2,2,4,128]{3,2,1,0:T(4,128)(2,1)S(1)}, bf16[2,2,4,128]{3,2,1,0:T(4,128)(2,1)S(1)}, u32[]{:S(2)}, u32[]{:S(2)}) collective-permute-start(bf16[2,2,4,128]{3,2,1,0:T(4,128)(2,1)S(1)} %bitcast.178), channel_id=1, source_target_pairs={{0,16},{4,20},{8,24},{12,28},{16,0},{20,4},{24,8},{28,12},{1,17},{... | collective-permute-start | bytes 12296 | tf_op jit(solution)/shard_map/ppermute | solution.py:159
  43.2 5.4 %collective-permute-start.12 = (bf16[2,2,4,128]{3,2,1,0:T(4,128)(2,1)S(1)}, bf16[2,2,4,128]{3,2,1,0:T(4,128)(2,1)S(1)}, u32[]{:S(2)}, u32[]{:S(2)}) collective-permute-start(bf16[2,2,4,128]{3,2,1,0:T(4,128)(2,1)S(1)} %bitcast.177), channel_id=1, source_target_pairs={{0,20},{4,16},{8,28},{12,24},{16,4},{20,0},{24,12},{28,8},{1,21},{... | collective-permute-start | bytes 12296 | tf_op jit(solution)/shard_map/ppermute | solution.py:159
  44.6 5.5 %collective-permute-start.13 = (bf16[2,2,4,128]{3,2,1,0:T(4,128)(2,1)S(1)}, bf16[2,2,4,128]{3,2,1,0:T(4,128)(2,1)S(1)}, u32[]{:S(2)}, u32[]{:S(2)}) collective-permute-start(bf16[2,2,4,128]{3,2,1,0:T(4,128)(2,1)S(1)} %bitcast.181), channel_id=1, source_target_pairs={{0,24},{4,28},{8,16},{12,20},{16,8},{20,12},{24,0},{28,4},{1,25},{... | collective-permute-start | bytes 12296 | tf_op jit(solution)/shard_map/ppermute | solution.py:159
  48.3 6.4 %collective-permute-start.14 = (bf16[2,2,4,128]{3,2,1,0:T(4,128)(2,1)S(1)}, bf16[2,2,4,128]{3,2,1,0:T(4,128)(2,1)S(1)}, u32[]{:S(2)}, u32[]{:S(2)}) collective-permute-start(bf16[2,2,4,128]{3,2,1,0:T(4,128)(2,1)S(1)} %bitcast.180), channel_id=1, source_target_pairs={{0,28},{4,24},{8,20},{12,16},{16,12},{20,8},{24,4},{28,0},{1,29},{... | collective-permute-start | bytes 12296 | tf_op jit(solution)/shard_map/ppermute | solution.py:159
  56.4 0.7 copy-start.5
  56.5 0.7 copy-start.4
  57.2 7.4 %collective-permute-start.16 = (f32[1,1,20,256]{3,2,1,0:T(8,128)S(1)}, f32[1,1,20,256]{3,2,1,0:T(8,128)S(1)}, u32[]{:S(2)}, u32[]{:S(2)}) collective-permute-start(f32[1,1,20,256]{3,2,1,0:T(8,128)S(1)} %bitcast.164), channel_id=1, source_target_pairs={{4,0},{8,4},{12,8},{16,12},{20,16},{24,20},{28,24},{5,1},{9,5},{13... | collective-permute-start | bytes 61448 | tf_op jit(solution)/shard_map/ppermute | solution.py:36
  58.5 6.1 %collective-permute-start.15 = (f32[1,1,20,256]{3,2,1,0:T(8,128)S(1)}, f32[1,1,20,256]{3,2,1,0:T(8,128)S(1)}, u32[]{:S(2)}, u32[]{:S(2)}) collective-permute-start(f32[1,1,20,256]{3,2,1,0:T(8,128)S(1)} %bitcast.165), channel_id=1, source_target_pairs={{0,4},{4,8},{8,12},{12,16},{16,20},{20,24},{24,28},{1,5},{5,9},{9,... | collective-permute-start | bytes 61448 | tf_op jit(solution)/shard_map/ppermute | solution.py:34
  64.6 4.4 %collective-permute-start.18 = (f32[1,3,20,256]{3,0,2,1:T(1,128)S(1)}, f32[1,3,20,256]{3,0,2,1:T(1,128)S(1)}, u32[]{:S(2)}, u32[]{:S(2)}) collective-permute-start(f32[1,3,20,256]{3,0,2,1:T(1,128)S(1)} %constant_dynamic-update-slice_fusion.8), channel_id=1, source_target_pairs={{1,0},{2,1},{3,2},{5,4},{6,5},{7,6},{9,8},{10,9},{11,10},{13,12},{... | collective-permute-start | bytes 184328 | tf_op jit(solution)/shard_map/ppermute | solution.py:36
  66.6 5.5 %collective-permute-start.17 = (f32[1,3,20,256]{3,0,2,1:T(1,128)S(1)}, f32[1,3,20,256]{3,0,2,1:T(1,128)S(1)}, u32[]{:S(2)}, u32[]{:S(2)}) collective-permute-start(f32[1,3,20,256]{3,0,2,1:T(1,128)S(1)} %constant_dynamic-update-slice_fusion.8), channel_id=1, source_target_pairs={{0,1},{1,2},{2,3},{4,5},{5,6},{6,7},{8,9},{9,10},{10,11},{12,13},{... | collective-permute-start | bytes 184328 | tf_op jit(solution)/shard_map/ppermute | solution.py:34
